TPU v7x, 32 devices: a whole 2x2x4 slice. The times are simulated.
32 devices in a mesh: rt: 8 (over y, x, core), ct: 4 (over z).
Axes of the slice: x: 2, y: 2, z: 4, core: 2. Of those that a mesh axis runs over, the one named last changes fastest.
Arguments:
- factor_rows: float32 [48, 2, 1024, 1024], P('rt', None, 'ct'), as said below
- slot_row: int32 [48], replicated, may hold values from -1 to 31, as said below
- known: float32 [48, 1024, 256], P('rt', 'ct'), may hold values from -6 to 6
- rhs: float32 [2, 1024, 256], P(None, 'ct', 'rt'), may hold values from -6 to 6
Outputs:
- solved: float32 [2, 1024, 256], P(None, 'ct', 'rt')
Inputs may be any that keep to these rules, and one draw needn't show every extreme that they name: `slot_row`: each row tile 0 to 31 stands in exactly one slot; the other slots hold -1. The slots of one index of rt are the 6 consecutive ones; at most 6 are live, and some index of rt has all 6 live. `factor_rows`: diagonal tiles L[0, 0] and L[1, 1] are lower triangular with diagonal entries from 1 to 2; the entry block (0, 1) is zero; entries of empty slots are arbitrary.
All inputs are finite; a program needn't handle non-finite values.
Results may differ from a plain program's by a relative error of at most 0.0003.
Values sent between devices are 32-bit elements; how exact they have to be, the bound alone decides.
No kernel may reach another device: no remote copies, remote signals or barrier semaphores. Data moves between devices by JAX's collectives and lax.ppermute only.
A program may use at most 64 MiB of HBM per device.

v0:
```python
import jax
import jax.numpy as jnp
from jax import lax
from jax.sharding import PartitionSpec as P


def spread(value, axis, root):
    mine = lax.axis_index(axis) == root
    return lax.psum(jnp.where(mine, value, jnp.zeros_like(value)), axis)


def shards(factor_rows, slot_row, known, rhs):
    high = lax.Precision.HIGHEST
    band = known.shape[1]
    columns = rhs.shape[2]
    slot_count = factor_rows.shape[0]
    offset = lax.axis_index("ct") * band
    col_offset = lax.axis_index("rt") * columns
    local_rows = lax.dynamic_slice_in_dim(
        slot_row, lax.axis_index("rt") * slot_count, slot_count, 0
    )
    live = (local_rows >= 2).astype(jnp.float32)
    masked = known * live[:, None, None]
    partial_value = jnp.einsum("scka,skr->car", factor_rows, masked, precision=high)
    pick_zero = local_rows == 0
    pick_one = local_rows == 1
    diag_zero = jnp.sum(jnp.where(pick_zero[:, None, None], factor_rows[:, 0], 0.0), 0)
    diag_one = jnp.sum(jnp.where(pick_one[:, None, None], factor_rows[:, 1], 0.0), 0)
    lower_one = jnp.sum(jnp.where(pick_one[:, None, None], factor_rows[:, 0], 0.0), 0)
    owner_zero = jnp.argmax(slot_row == 0) // slot_count
    owner_one = jnp.argmax(slot_row == 1) // slot_count
    tile_zero = spread(diag_zero, "rt", owner_zero)
    tile_one, tile_lower = (spread(diag_one, "rt", owner_one), spread(lower_one, "rt", owner_one))
    total = lax.psum(partial_value, ("rt", "ct"))
    rows_mine = lax.dynamic_slice_in_dim(total, offset, band, 1)
    mine = lax.dynamic_slice_in_dim(rows_mine, col_offset, columns, 2)
    residual = lax.all_gather(rhs - mine, "ct", axis=1, tiled=True)
    whole_zero, whole_one = (
        lax.all_gather(tile_zero, "ct", axis=0, tiled=True),
        lax.all_gather(tile_one, "ct", axis=0, tiled=True),
    )
    solved_one = lax.linalg.triangular_solve(
        whole_one, residual[1], left_side=True, lower=True, transpose_a=True
    )
    one_band = lax.dynamic_slice_in_dim(solved_one, offset, band, 0)
    coupling = jnp.einsum("ka,kr->ar", tile_lower, one_band, precision=high)
    coupled = lax.psum(coupling, "ct")
    solved_zero = lax.linalg.triangular_solve(
        whole_zero, residual[0] - coupled, left_side=True, lower=True, transpose_a=True
    )
    zero_band = lax.dynamic_slice_in_dim(solved_zero, offset, band, 0)
    return jnp.stack([zero_band, one_band])


def solution(mesh):
    in_specs = (P("rt", None, "ct", None), P(), P("rt", "ct", None), P(None, "ct", "rt"))
    out_specs = P(None, "ct", "rt")
    return jax.shard_map(shards, mesh=mesh, in_specs=in_specs, out_specs=out_specs, check_vma=False)
```

profile of v0, /device:TPU:0, one launch (start us, length us, event | category | flops | bytes accessed | tf_op | source)
XLA Modules:
  0.0 562.1 jit_solution(5160775739267857526)
XLA Ops:
  6.5 1.4 compare_reduce_fusion
  10.0 1.4 compare_reduce_fusion.1
  13.5 0.7 compare_convert_fusion
  14.2 6.1 %fusion.2 = (f32[256,1024]{1,0:T(8,128)S(1)}, f32[256,1024]{1,0:T(8,128)S(1)}, f32[256,1024]{1,0:T(8,128)S(1)}) fusion(f32[6,2,256,1024]{3,2,1,0:T(8,128)} %param.6, pred[6]{0:T(512)(128)(4,1)S(1)} %get-tuple-element.53, pred[6]{0:T(512)(128)(4,1)S(1)} %get-tuple-element.54), kind=kLoop, calls=%fused_computation.9 | loop fusion | flops 8650752 | bytes 15728652 | tf_op jit(solution)/shard_map/reduce_sum | solution.py:29
  20.3 1.1 broadcast_select_fusion.2
  21.4 1.6 broadcast_select_fusion
  23.3 14.9 %convolution_bitcast_fusion = f32[2,1024,256]{1,2,0:T(8,128)} fusion(f32[6,2,256,1024]{3,2,1,0:T(8,128)} %param.6, f32[6,256,256]{2,1,0:T(8,128)S(1)} %copy-done, f32[6]{0:T(128)S(1)} %get-tuple-element.52), kind=kOutput, calls=%fused_computation.13 | convolution fusion | flops 9664069632 | bytes 16252952 | tf_op jit(solution)/shard_map/scka,skr->car/dot_general | solution.py:24
  38.3 57.5 %all-reduce.9.cloned.1.call-done = (f32[256,1024]{1,0:T(8,128)}, f32[256,1024]{1,0:T(8,128)}, f32[256,1024]{1,0:T(8,128)}) async-done(((f32[256,1024]{1,0:T(8,128)}, f32[256,1024]{1,0:T(8,128)}, f32[256,1024]{1,0:T(8,128)}), (f32[256,1024]{1,0:T(8,128)}, f32[256,1024]{1,0:T(8,128)}, f32[256,1024]{1,0:T(8,128)})) %all-reduce.9.cloned.1.call-update) | async-done | bytes 3145744 | tf_op jit(solution)/shard_map/psum | solution.py:9
  95.9 140.0 %all-reduce.5.cloned.1.call-done = f32[2,1024,256]{1,2,0:T(8,128)} async-done(((f32[2,1024,256]{1,2,0:T(8,128)}), f32[2,1024,256]{1,2,0:T(8,128)}) %all-reduce.5.cloned.1.call-update) | async-done | bytes 2097168 | tf_op jit(solution)/shard_map/psum | solution.py:34
  235.9 1.0 dynamic-slice_subtract_fusion
  236.9 14.7 %all_gather.10 = f32[2,1024,32]{1,2,0:T(8,128)S(1)} all-gather(f32[2,256,32]{1,2,0:T(8,128)S(1)} %dynamic-slice_subtract_fusion), channel_id=1, replica_groups=mesh['rt'=8,'ct'=4] {'ct'}, dimensions={1}, use_global_device_ids=true | all-gather | bytes 327680 | tf_op jit(solution)/shard_map/all_gather | solution.py:37
  251.8 66.0 %all-gather.5.cloned.1.call-done = f32[1024,1024]{1,0:T(8,128)} async-done(((f32[256,1024]{1,0:T(8,128)}), f32[1024,1024]{1,0:T(8,128)}) %all-gather.5.cloned.1.call-update) | async-done | bytes 4194320 | tf_op jit(solution)/shard_map/all_gather | solution.py:40
  317.8 4.7 fusion.3
  322.6 22.5 %while.4 = (s32[]{:T(128)}, f32[1024,1024]{1,0:T(8,128)}, s32[8,2]{0,1:T(2,128)S(1)}, f32[8,128,128]{2,1,0:T(8,128)S(1)}, s32[]{:T(128)}) while((s32[]{:T(128)}, f32[1024,1024]{1,0:T(8,128)}, s32[8,2]{0,1:T(2,128)S(1)}, f32[8,128,128]{2,1,0:T(8,128)S(1)}, s32[]{:T(128)}) %tuple.49), condition=%wide.while_cond, body=%wide.while_body.sunk | while | flops 2 | bytes 131181 | solution.py:42
  323.2 2.2 bitcast_dynamic-update-slice_fusion.4
  325.5 0.5 fusion.106
  326.1 2.2 bitcast_dynamic-update-slice_fusion.4
  328.4 0.5 fusion.106
  328.9 2.2 bitcast_dynamic-update-slice_fusion.4
  331.2 0.5 fusion.106
  331.7 2.2 bitcast_dynamic-update-slice_fusion.4
  334.0 0.5 fusion.106
  334.5 2.2 bitcast_dynamic-update-slice_fusion.4
  337.3 2.2 bitcast_dynamic-update-slice_fusion.4
  340.2 2.2 bitcast_dynamic-update-slice_fusion.4
  342.5 0.5 fusion.106
  343.0 2.1 bitcast_dynamic-update-slice_fusion.4
  345.1 78.6 %custom-call.4 = f32[8,128,128]{1,2,0:T(8,128)S(1)} custom-call(f32[8,128,128]{2,1,0:T(8,128)S(1)} %get-tuple-element.24), custom_call_target="InvertDiagBlocksLowerTriangular" | custom-call | tf_op jit(solution)/shard_map/triangular_solve/custom-call.1 | solution.py:42
  423.9 1.0 convolution_subtract_fusion.7
  425.2 1.1 convolution_subtract_fusion.6
  426.5 1.2 convolution_subtract_fusion.5
  427.9 1.2 convolution_subtract_fusion.4
  429.4 1.3 convolution_subtract_fusion.13
  431.0 1.3 convolution_subtract_fusion.12
  432.6 1.4 convolution_subtract_fusion.11
  434.3 1.4 fusion.67
  435.8 4.7 fusion.4
  440.5 24.2 %while.5 = (s32[]{:T(128)}, f32[1024,1024]{1,0:T(8,128)}, s32[8,2]{0,1:T(2,128)S(1)}, f32[8,128,128]{2,1,0:T(8,128)S(1)}, s32[]{:T(128)}) while((s32[]{:T(128)}, f32[1024,1024]{1,0:T(8,128)}, s32[8,2]{0,1:T(2,128)S(1)}, f32[8,128,128]{2,1,0:T(8,128)S(1)}, s32[]{:T(128)}) %tuple.66), condition=%wide.while_cond.clone, body=%wide.while_body.clone.sunk | while | flops 2 | bytes 131181 | solution.py:48
  440.6 0.6 fusion.107
  441.2 2.3 bitcast_dynamic-update-slice_fusion.5
  443.6 0.6 fusion.107
  444.2 2.3 bitcast_dynamic-update-slice_fusion.5
  446.7 0.6 fusion.107
  447.3 2.3 bitcast_dynamic-update-slice_fusion.5
  449.7 0.6 fusion.107
  450.3 2.3 bitcast_dynamic-update-slice_fusion.5
  452.7 0.6 fusion.107
  453.3 2.3 bitcast_dynamic-update-slice_fusion.5
  455.8 0.6 fusion.107
  456.4 2.3 bitcast_dynamic-update-slice_fusion.5
  458.8 0.6 fusion.107
  459.4 2.3 bitcast_dynamic-update-slice_fusion.5
  461.8 0.6 fusion.107
  462.4 2.3 bitcast_dynamic-update-slice_fusion.5
  464.7 78.6 %custom-call.5 = f32[8,128,128]{1,2,0:T(8,128)S(1)} custom-call(f32[8,128,128]{2,1,0:T(8,128)S(1)} %get-tuple-element.25), custom_call_target="InvertDiagBlocksLowerTriangular" | custom-call | tf_op jit(solution)/shard_map/triangular_solve/custom-call.1 | solution.py:48
  543.3 0.9 fusion.20
  544.5 1.0 convolution_subtract_fusion.3
  545.7 1.1 convolution_subtract_fusion.2
  547.0 1.2 convolution_subtract_fusion.1
  548.4 1.2 convolution_subtract_fusion
  550.0 1.3 convolution_subtract_fusion.10
  551.5 1.3 convolution_subtract_fusion.9
  553.2 1.4 convolution_subtract_fusion.8
  554.9 0.6 pad_maximum_fusion
  (104 shorter events, 6.9 us)
Async XLA Ops:
  6.5 89.3 %all-reduce.9.cloned.1.call-start = ((), (), s32[]{:S(2)}) async-start(), calls=%async_computation.4 | async-start | bytes 6291456 | tf_op jit(solution)/shard_map/psum | solution.py:9
  21.4 1.9 copy-start
  23.1 212.8 %all-reduce.5.cloned.1.call-start = ((), (), s32[]{:S(2)}) async-start(), calls=%async_computation.1 | async-start | bytes 4194304 | tf_op jit(solution)/shard_map/psum | solution.py:34
  23.3 212.6 %copy-start.2 = (f32[2,256,32]{1,2,0:T(8,128)S(1)}, f32[2,256,32]{1,2,0:T(8,128)}, u32[]{:S(2)}) copy-start(f32[2,256,32]{1,2,0:T(8,128)} %param.9) | copy-start | bytes 196612
  38.2 279.6 %all-gather.5.cloned.1.call-start = ((), (), s32[]{:S(2)}) async-start(), calls=%async_computation.2 | async-start | bytes 5242880 | tf_op jit(solution)/shard_map/all_gather | solution.py:40
  95.8 339.9 %all-gather.3.cloned.1.call-start = ((), (), s32[]{:S(2)}) async-start(), calls=%async_computation | async-start | bytes 5242880 | tf_op jit(solution)/shard_map/all_gather | solution.py:39
  251.6 291.7 %all-reduce.7.cloned.1.call-start = ((), (), s32[]{:S(2)}) async-start(), calls=%async_computation.3 | async-start | bytes 262144 | tf_op jit(solution)/shard_map/psum | solution.py:47
  322.6 111.8 %copy-start.1 = (f32[256,1024]{1,0:T(8,128)S(1)}, f32[256,1024]{1,0:T(8,128)}, u32[]{:S(2)}) copy-start(f32[256,1024]{1,0:T(8,128)} %get-tuple-element.47) | copy-start | bytes 3145732
Sparse Core Ops, SparseCore 0:
  23.2 72.5 all-reduce.8
  102.0 133.8 all-reduce.4
  237.5 80.3 all-gather.4
  319.2 79.3 all-gather.2
  435.9 33.0 all-reduce.6
where the time goes:
time: 564 us; the launch traced here: 562 us
  waiting for transfers between devices  264 us (47%)
  other arithmetic  182 us (32%)
  local copies, waits for them, and re-layouts  47 us (8%)
  matrix products  36.6 us (6%)
  between operations  18 us (3%)
  blocking collectives  14.7 us (3%)
    psum x1, waiting for transfers between devices, shards(): total = lax.psum(partial_value, ('rt', 'ct'))  140 us
    another operation x3, other arithmetic, shards(): lax.linalg.triangular_solve(whole_zero, residual[0] - coupled, left_side=...  83.3 us
    another operation x2, other arithmetic, shards(): lax.linalg.triangular_solve(whole_one, residual[1], left_side=True, lower...  83.3 us
    all_gather x1, waiting for transfers between devices, shards(): lax.all_gather(tile_one, 'ct', axis=0, tiled=True)  66 us
    psum x1, waiting for transfers between devices, spread(): return lax.psum(jnp.where(mine, value, jnp.zeros_like(value)), axis)  57.5 us
    another operation x31, local copies, waits for them, and re-layouts, shards(): lax.linalg.triangular_solve(whole_zero, residual[0] - coupled, left_side=...  24.1 us
    another operation x28, local copies, waits for them, and re-layouts, shards(): lax.linalg.triangular_solve(whole_one, residual[1], left_side=True, lower...  22.4 us
    dot_general x1, matrix products, shards(): jnp.einsum('scka,skr->car', factor_rows, masked, precision=high)  14.9 us
  transfers between devices with their start and end apart: 5, of which 3 were waited for; matrix products, arithmetic and copies ran while one was open for 43% of the time, Pallas kernels for 0%

commit v1 on v0

--- a/solution.py
+++ b/solution.py
@@ -34,7 +34,23 @@
     total = lax.psum(partial_value, ("rt", "ct"))
     rows_mine = lax.dynamic_slice_in_dim(total, offset, band, 1)
     mine = lax.dynamic_slice_in_dim(rows_mine, col_offset, columns, 2)
-    residual = lax.all_gather(rhs - mine, "ct", axis=1, tiled=True)
+    value_2 = rhs - mine
+    ways, here, step = (lax.axis_size("ct"), lax.axis_index("ct"), value_2.shape[1])
+    dims = [n * ways if d == 1 else n for d, n in enumerate(value_2.shape)]
+    residual = lax.dynamic_update_slice_in_dim(
+        jnp.zeros(dims, value_2.dtype), value_2, here * step, axis=1
+    )
+    going_up = going_down = value_2
+    for far in range(1, ways // 2 + 1):
+        going_up = lax.ppermute(going_up, "ct", [(d, (d + 1) % ways) for d in range(ways)])
+        residual = lax.dynamic_update_slice_in_dim(
+            residual, going_up, (here - far) % ways * step, axis=1
+        )
+        if 2 * far < ways:
+            going_down = lax.ppermute(going_down, "ct", [(d, (d - 1) % ways) for d in range(ways)])
+            residual = lax.dynamic_update_slice_in_dim(
+                residual, going_down, (here + far) % ways * step, axis=1
+            )
     whole_zero, whole_one = (
         lax.all_gather(tile_zero, "ct", axis=0, tiled=True),
         lax.all_gather(tile_one, "ct", axis=0, tiled=True),

time: 564 us -> 563 us (level)
  blocking collectives: 14.7 us -> 0 us
  waiting for transfers between devices: 264 us -> 274 us
    all_gather x1 -> x0, blocking collectives: 14.7 us -> none  [shards(): residual = lax.all_gather(rhs - mine, 'ct', axis=1, tiled=True)]
    ppermute x0 -> x3, waiting for transfers between devices: none -> 8.51 us  [the longest x2 8.48 us: shards(): lax.ppermute(going_up, 'ct', [(d, (d + 1) % ways) for d in range(ways)])]
  transfers between devices with their start and end apart: 5 -> 8, of which waited for: 3 -> 5; matrix products, arithmetic and copies ran while one was open for 43% -> 43% of each run, Pallas kernels for 0% -> 0%
where the time goes in v1:
time: 563 us; the launch traced here: 562 us
  waiting for transfers between devices  274 us (49%)
  other arithmetic  182 us (32%)
  local copies, waits for them, and re-layouts  47 us (8%)
  matrix products  36.6 us (7%)
  between operations  18.1 us (3%)
    psum x1, waiting for transfers between devices, shards(): total = lax.psum(partial_value, ('rt', 'ct'))  140 us
    another operation x3, other arithmetic, shards(): lax.linalg.triangular_solve(whole_zero, residual[0] - coupled, left_side=...  83.3 us
    another operation x2, other arithmetic, shards(): lax.linalg.triangular_solve(whole_one, residual[1], left_side=True, lower...  83.3 us
    all_gather x1, waiting for transfers between devices, shards(): lax.all_gather(tile_one, 'ct', axis=0, tiled=True)  67.8 us
    psum x1, waiting for transfers between devices, spread(): return lax.psum(jnp.where(mine, value, jnp.zeros_like(value)), axis)  57.5 us
    another operation x31, local copies, waits for them, and re-layouts, shards(): lax.linalg.triangular_solve(whole_zero, residual[0] - coupled, left_side=...  24.1 us
    another operation x28, local copies, waits for them, and re-layouts, shards(): lax.linalg.triangular_solve(whole_one, residual[1], left_side=True, lower...  22.4 us
    dot_general x1, matrix products, shards(): jnp.einsum('scka,skr->car', factor_rows, masked, precision=high)  14.9 us
  transfers between devices with their start and end apart: 8, of which 5 were waited for; matrix products, arithmetic and copies ran while one was open for 43% of the time, Pallas kernels for 0%

profile of v1, /device:TPU:0, one launch (start us, length us, event | category | flops | bytes accessed | tf_op | source)
XLA Modules:
  0.0 561.7 jit_solution(18231705297164485665)
XLA Ops:
  6.5 1.4 compare_reduce_fusion
  10.0 1.4 compare_reduce_fusion.1
  13.5 0.7 compare_convert_fusion
  14.2 6.1 %fusion.2 = (f32[256,1024]{1,0:T(8,128)S(1)}, f32[256,1024]{1,0:T(8,128)S(1)}, f32[256,1024]{1,0:T(8,128)S(1)}) fusion(f32[6,2,256,1024]{3,2,1,0:T(8,128)} %param.6, pred[6]{0:T(512)(128)(4,1)S(1)} %get-tuple-element.55, pred[6]{0:T(512)(128)(4,1)S(1)} %get-tuple-element.56), kind=kLoop, calls=%fused_computation.9 | loop fusion | flops 8650752 | bytes 15728652 | tf_op jit(solution)/shard_map/reduce_sum | solution.py:29
  20.3 1.1 broadcast_select_fusion.2
  21.4 1.6 broadcast_select_fusion
  23.3 14.9 %convolution_bitcast_fusion = f32[2,1024,256]{1,2,0:T(8,128)} fusion(f32[6,2,256,1024]{3,2,1,0:T(8,128)} %param.6, f32[6,256,256]{2,1,0:T(8,128)S(1)} %copy-done, f32[6]{0:T(128)S(1)} %get-tuple-element.54), kind=kOutput, calls=%fused_computation.13 | convolution fusion | flops 9664069632 | bytes 16252952 | tf_op jit(solution)/shard_map/scka,skr->car/dot_general | solution.py:24
  38.3 57.5 %all-reduce.9.cloned.1.call-done = (f32[256,1024]{1,0:T(8,128)}, f32[256,1024]{1,0:T(8,128)}, f32[256,1024]{1,0:T(8,128)}) async-done(((f32[256,1024]{1,0:T(8,128)}, f32[256,1024]{1,0:T(8,128)}, f32[256,1024]{1,0:T(8,128)}), (f32[256,1024]{1,0:T(8,128)}, f32[256,1024]{1,0:T(8,128)}, f32[256,1024]{1,0:T(8,128)})) %all-reduce.9.cloned.1.call-update) | async-done | bytes 3145744 | tf_op jit(solution)/shard_map/psum | solution.py:9
  96.0 139.9 %all-reduce.5.cloned.1.call-done = f32[2,1024,256]{1,2,0:T(8,128)} async-done(((f32[2,1024,256]{1,2,0:T(8,128)}), f32[2,1024,256]{1,2,0:T(8,128)}) %all-reduce.5.cloned.1.call-update) | async-done | bytes 2097168 | tf_op jit(solution)/shard_map/psum | solution.py:34
  235.9 1.0 constant_dynamic-update-slice_fusion.53
  236.9 1.4 collective-permute-start
  238.3 2.5 collective-permute-start.1
  240.8 2.4 collective-permute-done
  243.3 6.1 %collective-permute-done.2 = f32[2,256,32]{1,2,0:T(8,128)S(1)} collective-permute-done((f32[2,256,32]{1,2,0:T(8,128)S(1)}, f32[2,256,32]{1,2,0:T(8,128)S(1)}, u32[]{:S(2)}, u32[]{:S(2)}) %collective-permute-start.2) | collective-permute-done | bytes 65568 | tf_op jit(solution)/shard_map/ppermute | solution.py:45
  249.7 67.8 %all-gather.5.cloned.1.call-done = f32[1024,1024]{1,0:T(8,128)} async-done(((f32[256,1024]{1,0:T(8,128)}), f32[1024,1024]{1,0:T(8,128)}) %all-gather.5.cloned.1.call-update) | async-done | bytes 4194320 | tf_op jit(solution)/shard_map/all_gather | solution.py:56
  317.5 4.7 fusion.3
  322.3 22.5 %while.4 = (s32[]{:T(128)}, f32[1024,1024]{1,0:T(8,128)}, s32[8,2]{0,1:T(2,128)S(1)}, f32[8,128,128]{2,1,0:T(8,128)S(1)}, s32[]{:T(128)}) while((s32[]{:T(128)}, f32[1024,1024]{1,0:T(8,128)}, s32[8,2]{0,1:T(2,128)S(1)}, f32[8,128,128]{2,1,0:T(8,128)S(1)}, s32[]{:T(128)}) %tuple.50), condition=%wide.while_cond, body=%wide.while_body.sunk | while | flops 2 | bytes 131181 | solution.py:58
  322.4 0.5 fusion.106
  322.9 2.2 bitcast_dynamic-update-slice_fusion.4
  325.7 2.2 bitcast_dynamic-update-slice_fusion.4
  328.0 0.5 fusion.106
  328.6 2.2 bitcast_dynamic-update-slice_fusion.4
  331.4 2.2 bitcast_dynamic-update-slice_fusion.4
  334.2 2.2 bitcast_dynamic-update-slice_fusion.4
  337.0 2.2 bitcast_dynamic-update-slice_fusion.4
  339.8 2.2 bitcast_dynamic-update-slice_fusion.4
  342.7 2.1 bitcast_dynamic-update-slice_fusion.4
  344.8 78.6 %custom-call.4 = f32[8,128,128]{1,2,0:T(8,128)S(1)} custom-call(f32[8,128,128]{2,1,0:T(8,128)S(1)} %get-tuple-element.24), custom_call_target="InvertDiagBlocksLowerTriangular" | custom-call | tf_op jit(solution)/shard_map/triangular_solve/custom-call.1 | solution.py:58
  423.6 1.0 fusion.43
  424.8 1.1 fusion.30
  426.2 1.2 fusion.26
  427.6 1.2 fusion.22
  429.1 1.3 fusion.18
  430.7 1.3 fusion.14
  432.3 1.4 fusion.10
  434.0 1.4 fusion.81
  435.4 4.7 fusion.4
  440.2 24.2 %while.5 = (s32[]{:T(128)}, f32[1024,1024]{1,0:T(8,128)}, s32[8,2]{0,1:T(2,128)S(1)}, f32[8,128,128]{2,1,0:T(8,128)S(1)}, s32[]{:T(128)}) while((s32[]{:T(128)}, f32[1024,1024]{1,0:T(8,128)}, s32[8,2]{0,1:T(2,128)S(1)}, f32[8,128,128]{2,1,0:T(8,128)S(1)}, s32[]{:T(128)}) %tuple.67), condition=%wide.while_cond.clone, body=%wide.while_body.clone.sunk | while | flops 2 | bytes 131181 | solution.py:64
  440.3 0.6 fusion.107
  440.9 2.3 bitcast_dynamic-update-slice_fusion.5
  443.3 0.6 fusion.107
  443.9 2.3 bitcast_dynamic-update-slice_fusion.5
  446.3 0.6 fusion.107
  446.9 2.3 bitcast_dynamic-update-slice_fusion.5
  449.4 0.6 fusion.107
  450.0 2.3 bitcast_dynamic-update-slice_fusion.5
  452.4 0.6 fusion.107
  453.0 2.3 bitcast_dynamic-update-slice_fusion.5
  455.4 0.6 fusion.107
  456.0 2.3 bitcast_dynamic-update-slice_fusion.5
  458.5 0.6 fusion.107
  459.1 2.3 bitcast_dynamic-update-slice_fusion.5
  461.5 0.6 fusion.107
  462.1 2.3 bitcast_dynamic-update-slice_fusion.5
  464.4 78.6 %custom-call.5 = f32[8,128,128]{1,2,0:T(8,128)S(1)} custom-call(f32[8,128,128]{2,1,0:T(8,128)S(1)} %get-tuple-element.25), custom_call_target="InvertDiagBlocksLowerTriangular" | custom-call | tf_op jit(solution)/shard_map/triangular_solve/custom-call.1 | solution.py:64
  543.0 0.9 fusion.32
  544.1 1.0 fusion.34
  545.4 1.1 fusion.28
  546.7 1.2 fusion.24
  548.1 1.2 fusion.20
  549.6 1.3 fusion.16
  551.2 1.3 fusion.12
  552.8 1.4 fusion.8
  554.6 0.6 pad_maximum_fusion
  (113 shorter events, 8.7 us)
Async XLA Ops:
  6.5 89.3 %all-reduce.9.cloned.1.call-start = ((), (), s32[]{:S(2)}) async-start(), calls=%async_computation.4 | async-start | bytes 6291456 | tf_op jit(solution)/shard_map/psum | solution.py:9
  21.4 1.9 copy-start
  23.1 212.8 %all-reduce.5.cloned.1.call-start = ((), (), s32[]{:S(2)}) async-start(), calls=%async_computation.1 | async-start | bytes 4194304 | tf_op jit(solution)/shard_map/psum | solution.py:34
  23.3 212.6 %copy-start.2 = (f32[2,256,32]{1,2,0:T(8,128)S(1)}, f32[2,256,32]{1,2,0:T(8,128)}, u32[]{:S(2)}) copy-start(f32[2,256,32]{1,2,0:T(8,128)} %param.9) | copy-start | bytes 196612
  38.2 279.3 %all-gather.5.cloned.1.call-start = ((), (), s32[]{:S(2)}) async-start(), calls=%async_computation.2 | async-start | bytes 5242880 | tf_op jit(solution)/shard_map/all_gather | solution.py:56
  95.8 339.6 %all-gather.3.cloned.1.call-start = ((), (), s32[]{:S(2)}) async-start(), calls=%async_computation | async-start | bytes 5242880 | tf_op jit(solution)/shard_map/all_gather | solution.py:55
  236.9 6.3 %collective-permute-start = (f32[2,256,32]{1,2,0:T(8,128)S(1)}, f32[2,256,32]{1,2,0:T(8,128)S(1)}, u32[]{:S(2)}, u32[]{:S(2)}) collective-permute-start(f32[2,256,32]{1,2,0:T(8,128)S(1)} %get-tuple-element.49), channel_id=1, source_target_pairs={{0,1},{1,2},{2,3},{3,0},{4,5},{5,6},{6,7},{7,4},{8,9},{9,10},{10,1... | collective-permute-start | bytes 196616 | tf_op jit(solution)/shard_map/ppermute | solution.py:45
  238.3 5.0 collective-permute-start.1
  243.2 6.2 %collective-permute-start.2 = (f32[2,256,32]{1,2,0:T(8,128)S(1)}, f32[2,256,32]{1,2,0:T(8,128)S(1)}, u32[]{:S(2)}, u32[]{:S(2)}) collective-permute-start(f32[2,256,32]{1,2,0:T(8,128)S(1)} %collective-permute-done), channel_id=1, source_target_pairs={{0,1},{1,2},{2,3},{3,0},{4,5},{5,6},{6,7},{7,4},{8,9},{9,10},{10,1... | collective-permute-start | bytes 196616 | tf_op jit(solution)/shard_map/ppermute | solution.py:45
  249.5 293.5 %all-reduce.7.cloned.1.call-start = ((), (), s32[]{:S(2)}) async-start(), calls=%async_computation.3 | async-start | bytes 262144 | tf_op jit(solution)/shard_map/psum | solution.py:63
  322.2 111.8 %copy-start.1 = (f32[256,1024]{1,0:T(8,128)S(1)}, f32[256,1024]{1,0:T(8,128)}, u32[]{:S(2)}) copy-start(f32[256,1024]{1,0:T(8,128)} %get-tuple-element.47) | copy-start | bytes 3145732
Sparse Core Ops, SparseCore 0:
  23.2 72.5 all-reduce.8
  102.0 133.8 all-reduce.4
  237.5 79.9 all-gather.4
  318.9 78.9 all-gather.2
  435.5 32.6 all-reduce.6
